TPU v7x, 512 devices: a whole 4x8x8 slice. The times are simulated.
512 devices in a mesh: slab: 32 (over y, x), band: 16 (over z, core).
Axes of the slice: x: 4, y: 8, z: 8, core: 2. Of those that a mesh axis runs over, the one named last changes fastest.
Arguments:
- basis: float32 [3, 512, 49152], P(None, 'slab', 'band')
- offsets: float32 [3, 512, 256], P(None, 'slab', 'band'), may hold values from -0.45 to 0.45
- bond_modulus: float32 [512, 256], P('slab', 'band'), may hold values from 0.5 to 2
- bulk_modulus: float32 [512, 256], P('slab', 'band'), may hold values from 0.5 to 2
- springs: float32 [512, 256], P('slab', 'band'), may hold values from 0.5 to 2
- intact: int32 [32, 32, 9], P('slab', 'band'), may hold values from 0 to 1, as said below
Outputs:
- new_modes: float32 [3, 512, 16384], P(None, 'slab', 'band')
- new_images: float32 [3, 512, 16384], P(None, 'slab', 'band')
- reduced: float32 [64, 64], replicated
Inputs may be any that keep to these rules, and one draw needn't show every extreme that they name: intact[i, j, 3 (dx + 1) + (dy + 1)] is 1 where the bonds between block (i, j) and block (i + dx, j + dy) are intact, and 0 where they are broken or that block lies outside the plate; the entry for (0, 0) is always 1, and the entry for (dx, dy) of one block equals the entry for (-dx, -dy) of the other.
All inputs are finite; a program needn't handle non-finite values.
Results may differ from a plain program's by a relative error of at most 0.0003.
Values sent between devices are 32-bit elements; how exact they have to be, the bound alone decides.
No kernel may reach another device: no remote copies, remote signals or barrier semaphores. Data moves between devices by JAX's collectives and lax.ppermute only.
A program may use at most 128 MiB of HBM per device.

v0:
```python
import jax
import jax.numpy as jnp
from jax import lax
from jax.sharding import PartitionSpec as P

BLOCK_X = 16
BLOCK_Y = 8
REACH = 3
MODES = 64
NCOL = 192
horizon_square = 9.0
bond_scale = 1.0 / 18.0
dilation_scale = 1.0 / 27.0
highest = lax.Precision.HIGHEST


def padded(value, sides, width):
    for axis, dim in sides:
        size, length = (lax.axis_size(axis), value.shape[dim])
        up = [(i, (i + 1) % size) for i in range(size - 1)]
        down = [(j, i) for i, j in up]
        last = lax.slice_in_dim(value, length - width, length, axis=dim)
        first = lax.slice_in_dim(value, 0, width, axis=dim)
        before = lax.ppermute(last, axis, up)
        after = lax.ppermute(first, axis, down)
        value = jnp.concatenate([before, value, after], axis=dim)
    return value


def window(array, margin, region):
    start_x, count_x, start_y, count_y = region
    piece = array[
        :,
        start_x + margin : start_x + margin + count_x,
        start_y + margin : start_y + margin + count_y,
    ]
    return piece.reshape((piece.shape[0], count_x * count_y) + piece.shape[3:])


def widened(region):
    start_x, count_x, start_y, count_y = region
    return (start_x - REACH, count_x + 2 * REACH, start_y - REACH, count_y + 2 * REACH)


def lattice(region):
    start_x, count_x, start_y, count_y = region
    along_x = jnp.repeat(jnp.arange(start_x, start_x + count_x, dtype=jnp.int32), count_y)
    along_y = jnp.tile(jnp.arange(start_y, start_y + count_y, dtype=jnp.int32), count_x)
    return (along_x, along_y)


def pair_geometry(geometry, margin, region, bond_table, table_shift):
    home_geometry = window(geometry, margin, region)
    far_geometry = window(geometry, margin, widened(region))
    home_x, home_y = lattice(region)
    far_x, far_y = lattice(widened(region))
    home_block_x = jnp.floor_divide(home_x, BLOCK_X)
    home_block_y = jnp.floor_divide(home_y, BLOCK_Y)
    offset_code = 3 * (jnp.floor_divide(far_x, BLOCK_X)[None, :] - home_block_x[:, None] + 1) + (
        jnp.floor_divide(far_y, BLOCK_Y)[None, :] - home_block_y[:, None] + 1
    )
    select_rows = (
        home_block_x[:, None] + table_shift
        == jnp.arange(bond_table.shape[0], dtype=jnp.int32)[None, :]
    ).astype(jnp.float32)
    select_cols = (
        home_block_y[:, None] + table_shift
        == jnp.arange(bond_table.shape[1], dtype=jnp.int32)[None, :]
    ).astype(jnp.float32)
    home_bonds = jnp.einsum(
        "na,nb,abo->no", select_rows, select_cols, bond_table.astype(jnp.float32), precision=highest
    )
    intact_mask = jnp.zeros(offset_code.shape, jnp.float32)
    for offset in range(9):
        intact_mask = intact_mask + jnp.where(
            offset_code == offset, home_bonds[:, offset][:, None], 0.0
        )
    bond_vector = jnp.stack(
        [
            (far_x[None, :] - home_x[:, None]).astype(jnp.float32)
            + far_geometry[0][None, :]
            - home_geometry[0][:, None],
            (far_y[None, :] - home_y[:, None]).astype(jnp.float32)
            + far_geometry[1][None, :]
            - home_geometry[1][:, None],
            far_geometry[2][None, :] - home_geometry[2][:, None],
        ],
        axis=1,
    )
    distance = jnp.sum(bond_vector * bond_vector, axis=1)
    weight = jnp.maximum(1.0 - distance / horizon_square, 0.0) * intact_mask
    return (bond_vector, weight, home_geometry, far_geometry)


def volume_terms(tile_set, home_field, far_field):
    bond_vector, weight, home_geometry, far_geometry = tile_set
    home_count = bond_vector.shape[0]
    far_count = bond_vector.shape[2]
    weighted = weight[:, None, :] * bond_vector
    far_flat = far_field.reshape(3 * far_count, home_field.shape[2])
    volume_change = jnp.dot(
        weighted.reshape(home_count, 3 * far_count), far_flat, precision=highest
    )
    return volume_change - jnp.einsum(
        "nc,cnk->nk", jnp.sum(weighted, axis=2), home_field, precision=highest
    )


def bond_terms(tile_set, home_field, far_field):
    bond_vector, weight, home_geometry, far_geometry = tile_set
    home_count = bond_vector.shape[0]
    far_count = bond_vector.shape[2]
    column_count = home_field.shape[2]
    far_flat = far_field.reshape(3 * far_count, column_count)
    coupling = weight * (home_geometry[3][:, None] + far_geometry[3][None, :]) * bond_scale
    leading = jnp.transpose(bond_vector, (1, 0, 2))
    tensor = coupling[None, :, None, :] * leading[:, :, None, :] * bond_vector[None, :, :, :]
    bond_force = jnp.einsum("cnd,dnk->cnk", jnp.sum(tensor, axis=3), home_field, precision=highest)
    return bond_force - jnp.dot(
        tensor.reshape(3 * home_count, 3 * far_count), far_flat, precision=highest
    ).reshape(3, home_count, column_count)


def dilatation_terms(tile_set, home_value, far_value):
    bond_vector, weight, home_geometry, far_geometry = tile_set
    home_count = bond_vector.shape[0]
    weighted = jnp.transpose(weight[:, None, :] * bond_vector, (1, 0, 2))
    remote = jnp.dot(weighted.reshape(3 * home_count, -1), far_value, precision=highest).reshape(
        3, home_count, far_value.shape[1]
    )
    return -(remote + jnp.sum(weighted, axis=2)[:, :, None] * home_value[None, :, :])


def rotation(mass_gram, stiff_gram, mode_count):
    mass_factor = jnp.linalg.cholesky(mass_gram)
    left_solved = lax.linalg.triangular_solve(mass_factor, stiff_gram, left_side=True, lower=True)
    projected = lax.linalg.triangular_solve(mass_factor, left_solved.T, left_side=True, lower=True)
    projected = 0.5 * (projected + projected.T)
    stiff_factor = jnp.linalg.cholesky(projected)
    target = jnp.eye(stiff_gram.shape[0], mode_count, dtype=stiff_gram.dtype)
    forward = lax.linalg.triangular_solve(stiff_factor, target, left_side=True, lower=True)
    inverse = lax.linalg.triangular_solve(
        stiff_factor, forward, left_side=True, lower=True, transpose_a=True
    )
    normal = jnp.linalg.cholesky(jnp.dot(inverse.T, inverse, precision=highest))
    lifted = lax.linalg.triangular_solve(
        mass_factor, inverse, left_side=True, lower=True, transpose_a=True
    )
    return lax.linalg.triangular_solve(
        normal, lifted, left_side=False, lower=True, transpose_a=True
    )


def local(basis, offsets, bond_modulus, bulk_modulus, springs, intact):
    size_x = offsets.shape[1]
    size_y = offsets.shape[2]
    column_count = NCOL
    basis = basis.reshape(3, size_x, size_y, column_count)
    strip_count = intact.shape[0]
    strip_x = size_x // strip_count
    total_rows = float(3 * size_x * size_y * lax.axis_size("slab") * lax.axis_size("band"))
    flat_basis = basis.reshape(-1, column_count)
    strips = [(0, strip_x, 0, size_y)]
    margin = REACH
    geometry = jnp.concatenate([offsets, bond_modulus[None]], axis=0)
    wide_field, wide_geometry = (
        padded(basis, (("slab", 1), ("band", 2)), margin),
        padded(geometry, (("slab", 1), ("band", 2)), margin),
    )
    table_shift = 0
    tile_sets = [
        pair_geometry(wide_geometry, margin, region, intact, table_shift) for region in strips
    ]
    volumes = []
    forces = []
    for region, tile_set in zip(strips, tile_sets):
        home_field = window(wide_field, margin, region)
        far_field = window(wide_field, margin, widened(region))
        volumes.append(volume_terms(tile_set, home_field, far_field))
        forces.append(bond_terms(tile_set, home_field, far_field))
    volume_grid = jnp.concatenate(
        [volume.reshape(strip_x, size_y, column_count) for volume in volumes], axis=0
    )
    dilatation = dilation_scale * bulk_modulus[:, :, None] * volume_grid
    wide_dilatation = padded(dilatation, (("slab", 0), ("band", 1)), REACH)
    images = []
    for region, tile_set, bond_force in zip(strips, tile_sets, forces):
        home_value = window(wide_dilatation[None], REACH, region)[0]
        far_value = window(wide_dilatation[None], REACH, widened(region))[0]
        home_field = window(basis, 0, region)
        stiffness = window(springs[None], 0, region)[0]
        image_strip = (
            bond_force
            + dilatation_terms(tile_set, home_value, far_value)
            + stiffness[None, :, None] * home_field
        )
        images.append(image_strip.reshape(3, strip_x, size_y, column_count))
    image_grid = images[0]
    flat_images = image_grid.reshape(-1, column_count)
    stiff_part = jnp.einsum("rk,rl->kl", flat_basis, flat_images, precision=highest)
    mass_part = jnp.einsum("rk,rl->kl", flat_basis, flat_basis, precision=highest)
    mass_total, stiff_total = lax.psum((mass_part, stiff_part), ("slab", "band"))
    mass_gram = mass_total / total_rows
    stiff_gram = stiff_total / total_rows
    stiff_gram = 0.5 * (stiff_gram + stiff_gram.T)
    rotate = rotation(mass_gram, stiff_gram, MODES)
    new_modes = jnp.einsum("cxyk,km->cxym", basis, rotate, precision=highest)
    new_images = jnp.einsum("cxyk,km->cxym", image_grid, rotate, precision=highest)
    reduced = (
        lax.psum(
            jnp.einsum("cxym,cxyn->mn", new_modes, new_images, precision=highest), ("slab", "band")
        )
        / total_rows
    )
    return (
        new_modes.reshape(3, size_x, size_y * MODES),
        new_images.reshape(3, size_x, size_y * MODES),
        reduced,
    )


def solution(mesh):
    in_specs = (
        P(None, "slab", "band"),
        P(None, "slab", "band"),
        P("slab", "band"),
        P("slab", "band"),
        P("slab", "band"),
        P("slab", "band", None),
    )
    out_specs = (P(None, "slab", "band"), P(None, "slab", "band"), P())
    return jax.shard_map(local, mesh=mesh, in_specs=in_specs, out_specs=out_specs, check_vma=False)
```

profile of v0, /device:TPU:1, one launch (start us, length us, event | category | flops | bytes accessed | tf_op | source)
XLA Modules:
  0.0 619.2 jit_solution(15690530505633483698)
XLA Ops:
  9.4 4.6 collective-permute-start
  16.1 3.4 collective-permute-start.4
  27.8 7.3 %collective-permute-start.3 = (f32[4,22,3]{2,1,0:T(8,128)}, f32[4,22,3]{2,1,0:T(8,128)S(1)}, u32[]{:S(2)}, u32[]{:S(2)}) collective-permute-start(f32[4,22,3]{2,1,0:T(8,128)} %get-tuple-element.109), channel_id=1, source_target_pairs={{1,0},{2,1},{3,2},{4,3},{5,4},{6,5},{7,6},{8,7},{9,8},{10,9},{11,1... | collective-permute-start | bytes 3176 | tf_op jit(solution)/shard_map/ppermute | solution.py:25
  48.9 3.0 collective-permute-start.7
  58.1 2.8 pad_maximum_fusion
  63.5 4.4 convolution_subtract_fusion
  71.8 4.9 collective-permute-start.8
  76.7 4.3 fusion.87
  84.6 4.8 collective-permute-start.10
  89.5 4.3 fusion.19
  93.8 5.4 mul.174
  107.9 6.6 %fusion.10 = f32[3,256,192]{1,2,0:T(8,128)S(1)} fusion(f32[3,256,192]{1,2,0:T(8,128)S(1)} %fusion.16, f32[3,256,1452]{1,2,0:T(8,128)} %mul.174, f32[1452,192]{1,0:T(8,128)S(1)} %copy-done, f32[256,3,192]{0,2,1:T(8,128)S(1)} %copy-done.5, f32[3,256,192]{1,2,0:T(8,128)S(1)} %copy-done.6, f32[256]{0:T(256)S(1)} %copy-done.23), kind=kOutput, calls=%fused_computation.12 | convolution fusion | flops 2569863168 | bytes 7936000 | tf_op jit(solution)/shard_map/dot_general | solution.py:119
  117.0 275.1 %all-reduce.10.cloned.1.call-done = (f32[192,192]{1,0:T(8,128)}, f32[192,192]{1,0:T(8,128)}) async-done(((f32[192,192]{1,0:T(8,128)}, f32[192,192]{1,0:T(8,128)}), (f32[192,192]{1,0:T(8,128)}, f32[192,192]{1,0:T(8,128)})) %all-reduce.10.cloned.1.call-update) | async-done | bytes 294928 | tf_op jit(solution)/shard_map/psum | solution.py:202
  394.3 11.7 %cholesky.171 = f32[128,128]{1,0:T(8,128)S(1)} custom-call(f32[128,128]{1,0:T(8,128)S(1)} %copy.93), custom_call_target="Cholesky" | custom-call | tf_op jit(solution)/shard_map/jit(cholesky)/cholesky | solution.py:135
  406.1 10.2 %custom-call.28 = f32[1,128,128]{1,2,0:T(8,128)S(1)} custom-call(f32[1,128,128]{2,1,0:T(8,128)S(1)} %get-tuple-element.103), custom_call_target="InvertDiagBlocksLowerTriangular" | custom-call | tf_op jit(solution)/shard_map/jit(cholesky)/cholesky | solution.py:135
  416.8 5.9 cholesky.191
  425.6 19.7 %custom-call.33 = f32[2,128,128]{1,2,0:T(8,128)S(1)} custom-call(f32[2,128,128]{2,1,0:T(8,128)S(1)} %pad_maximum_fusion.4), custom_call_target="InvertDiagBlocksLowerTriangular" | custom-call | tf_op jit(solution)/shard_map/triangular_solve/custom-call.6 | solution.py:146
  447.5 11.7 %cholesky.209 = f32[128,128]{1,0:T(8,128)S(1)} custom-call(f32[128,128]{1,0:T(8,128)S(1)} %cholesky.246), custom_call_target="Cholesky" | custom-call | tf_op jit(solution)/shard_map/jit(cholesky)/cholesky | solution.py:139
  459.2 9.8 %custom-call.31 = f32[1,128,128]{1,2,0:T(8,128)S(1)} custom-call(f32[1,128,128]{2,1,0:T(8,128)S(1)} %get-tuple-element.101), custom_call_target="InvertDiagBlocksLowerTriangular" | custom-call | tf_op jit(solution)/shard_map/jit(cholesky)/cholesky | solution.py:139
  469.4 5.8 cholesky.229
  478.1 19.8 %custom-call.32 = f32[2,128,128]{1,2,0:T(8,128)S(1)} custom-call(f32[2,128,128]{2,1,0:T(8,128)S(1)} %pad_maximum_fusion.5), custom_call_target="InvertDiagBlocksLowerTriangular" | custom-call | tf_op jit(solution)/shard_map/triangular_solve/custom-call.6 | solution.py:142
  500.1 5.8 cholesky.98
  507.3 4.9 custom-call.24
  516.5 95.0 %psum.23 = f32[64,64]{1,0:T(8,128)S(1)} all-reduce(f32[64,64]{1,0:T(8,128)S(1)} %convolution_bitcast_fusion.3), channel_id=1, replica_groups=mesh['slab'=32,'band'=16] {'slab','band'}, use_global_device_ids=true, to_apply=%region_12.16 | all-reduce | flops 4096 | bytes 32768 | tf_op jit(solution)/shard_map/psum | solution.py:210
  (233 shorter events, 69.8 us)
Async XLA Ops:
  7.2 13.6 %copy-start.8 = (f32[3,16,16]{2,1,0:T(8,128)S(1)}, f32[3,16,16]{2,1,0:T(8,128)}, u32[]{:S(2)}) copy-start(f32[3,16,16]{2,1,0:T(8,128)} %param.12) | copy-start | bytes 9220
  7.2 14.2 %copy-start.3 = (f32[3,16,3072]{2,1,0:T(8,128)S(1)}, f32[3,16,3072]{2,1,0:T(8,128)}, u32[]{:S(2)}) copy-start(f32[3,16,3072]{2,1,0:T(8,128)} %param.11) | copy-start | bytes 1769476
  7.2 384.9 %all-reduce.10.cloned.1.call-start = ((), (), s32[]{:S(2)}) async-start(), calls=%async_computation | async-start | bytes 786432 | tf_op jit(solution)/shard_map/psum | solution.py:202
  8.1 19.1 %collective-permute-start.1 = (f32[4,3,16]{2,1,0:T(4,128)S(1)}, f32[4,3,16]{2,1,0:T(4,128)S(1)}, u32[]{:S(2)}, u32[]{:S(2)}) collective-permute-start(f32[4,3,16]{2,1,0:T(4,128)S(1)} %get-tuple-element.115), channel_id=1, source_target_pairs={{16,0},{32,16},{48,32},{64,48},{80,64},{96,80},{112,96},{128,112},... | collective-permute-start | bytes 2312 | tf_op jit(solution)/shard_map/ppermute | solution.py:25
  9.3 13.5 %copy-start.37 = (s32[1,2,9]{2,1,0:T(2,128)S(1)}, s32[1,2,9]{2,1,0:T(2,128)}, u32[]{:S(2)}) copy-start(s32[1,2,9]{2,1,0:T(2,128)} %param.16) | copy-start | bytes 220
  9.3 14.5 %copy-start.22 = (f32[16,16]{1,0:T(8,128)S(1)}, f32[16,16]{1,0:T(8,128)}, u32[]{:S(2)}) copy-start(f32[16,16]{1,0:T(8,128)} %param.14) | copy-start | bytes 3076
  9.4 17.8 %collective-permute-start = (f32[4,3,16]{2,1,0:T(4,128)S(1)}, f32[4,3,16]{2,1,0:T(4,128)S(1)}, u32[]{:S(2)}, u32[]{:S(2)}) collective-permute-start(f32[4,3,16]{2,1,0:T(4,128)S(1)} %get-tuple-element.114), channel_id=1, source_target_pairs={{0,16},{16,32},{32,48},{48,64},{64,80},{80,96},{96,112},{112,128},... | collective-permute-start | bytes 2312 | tf_op jit(solution)/shard_map/ppermute | solution.py:24
  15.4 32.4 %copy-start.1 = (f32[3,16,16,192]{3,2,1,0:T(8,128)}, f32[3,16,16,192]{3,2,1,0:T(8,128)S(1)}, u32[]{:S(2)}) copy-start(f32[3,16,16,192]{3,2,1,0:T(8,128)S(1)} %reshape.1000) | copy-start | bytes 1769476
  16.1 31.6 %collective-permute-start.4 = (f32[3,3,16,192]{3,2,1,0:T(8,128)}, f32[3,3,16,192]{3,2,1,0:T(8,128)S(1)}, u32[]{:S(2)}, u32[]{:S(2)}) collective-permute-start(f32[3,3,16,192]{3,2,1,0:T(8,128)} %get-tuple-element.93), channel_id=1, source_target_pairs={{0,16},{16,32},{32,48},{48,64},{64,80},{80,96},{96,112},{112,128},... | collective-permute-start | bytes 331784 | tf_op jit(solution)/shard_map/ppermute | solution.py:24
  19.5 28.3 %collective-permute-start.5 = (f32[3,3,16,192]{3,2,1,0:T(8,128)S(1)}, f32[3,3,16,192]{3,2,1,0:T(8,128)S(1)}, u32[]{:S(2)}, u32[]{:S(2)}) collective-permute-start(f32[3,3,16,192]{3,2,1,0:T(8,128)S(1)} %get-tuple-element.92), channel_id=1, source_target_pairs={{16,0},{32,16},{48,32},{64,48},{80,64},{96,80},{112,96},{128,112},... | collective-permute-start | bytes 331784 | tf_op jit(solution)/shard_map/ppermute | solution.py:25
  27.8 15.1 %collective-permute-start.3 = (f32[4,22,3]{2,1,0:T(8,128)}, f32[4,22,3]{2,1,0:T(8,128)S(1)}, u32[]{:S(2)}, u32[]{:S(2)}) collective-permute-start(f32[4,22,3]{2,1,0:T(8,128)} %get-tuple-element.109), channel_id=1, source_target_pairs={{1,0},{2,1},{3,2},{4,3},{5,4},{6,5},{7,6},{8,7},{9,8},{10,9},{11,1... | collective-permute-start | bytes 3176 | tf_op jit(solution)/shard_map/ppermute | solution.py:25
  35.1 7.7 %collective-permute-start.2 = (f32[4,22,3]{2,1,0:T(8,128)S(1)}, f32[4,22,3]{2,1,0:T(8,128)}, u32[]{:S(2)}, u32[]{:S(2)}) collective-permute-start(f32[4,22,3]{2,1,0:T(8,128)S(1)} %get-tuple-element.108), channel_id=1, source_target_pairs={{0,1},{1,2},{2,3},{3,4},{4,5},{5,6},{6,7},{7,8},{8,9},{9,10},{10,1... | collective-permute-start | bytes 3176 | tf_op jit(solution)/shard_map/ppermute | solution.py:24
  38.1 6.3 %copy-start.12 = (s32[484]{0:T(512)S(1)}, s32[484]{0:T(512)}, u32[]{:S(2)}) copy-start(s32[484]{0:T(512)} %copy-done.11) | copy-start | bytes 5812
  38.1 6.3 %copy-start.14 = (s32[484]{0:T(512)S(1)}, s32[484]{0:T(512)}, u32[]{:S(2)}) copy-start(s32[484]{0:T(512)} %copy-done.13) | copy-start | bytes 5812
  38.1 6.3 %copy-start.17 = (s32[256]{0:T(256)S(1)}, s32[256]{0:T(256)}, u32[]{:S(2)}) copy-start(s32[256]{0:T(256)} %copy-done.16) | copy-start | bytes 3076
  47.9 6.6 %copy-start.4 = (f32[3,22,16,192]{3,2,1,0:T(8,128)}, f32[3,22,16,192]{3,2,1,0:T(8,128)S(1)}, u32[]{:S(2)}) copy-start(f32[3,22,16,192]{3,2,1,0:T(8,128)S(1)} %constant_dynamic-update-slice_fusion) | copy-start | bytes 2433028
  48.9 8.1 %collective-permute-start.7 = (f32[3,22,3,192]{3,2,1,0:T(4,128)}, f32[3,22,3,192]{3,2,1,0:T(4,128)}, u32[]{:S(2)}, u32[]{:S(2)}) collective-permute-start(f32[3,22,3,192]{3,2,1,0:T(4,128)} %get-tuple-element.91), channel_id=1, source_target_pairs={{1,0},{2,1},{3,2},{4,3},{5,4},{6,5},{7,6},{8,7},{9,8},{10,9},{11,1... | collective-permute-start | bytes 456200 | tf_op jit(solution)/shard_map/ppermute | solution.py:25
  51.9 6.3 %collective-permute-start.6 = (f32[3,22,3,192]{3,2,1,0:T(4,128)}, f32[3,22,3,192]{3,2,1,0:T(4,128)}, u32[]{:S(2)}, u32[]{:S(2)}) collective-permute-start(f32[3,22,3,192]{3,2,1,0:T(4,128)} %get-tuple-element.90), channel_id=1, source_target_pairs={{0,1},{1,2},{2,3},{3,4},{4,5},{5,6},{6,7},{7,8},{8,9},{9,10},{10,1... | collective-permute-start | bytes 456200 | tf_op jit(solution)/shard_map/ppermute | solution.py:24
  70.5 11.5 %collective-permute-start.9 = (f32[3,16,192]{2,1,0:T(8,128)}, f32[3,16,192]{2,1,0:T(8,128)S(1)}, u32[]{:S(2)}, u32[]{:S(2)}) collective-permute-start(f32[3,16,192]{2,1,0:T(8,128)} %get-tuple-element.99), channel_id=1, source_target_pairs={{16,0},{32,16},{48,32},{64,48},{80,64},{96,80},{112,96},{128,112},... | collective-permute-start | bytes 110600 | tf_op jit(solution)/shard_map/ppermute | solution.py:25
  71.8 10.2 %collective-permute-start.8 = (f32[3,16,192]{2,1,0:T(8,128)S(1)}, f32[3,16,192]{2,1,0:T(8,128)S(1)}, u32[]{:S(2)}, u32[]{:S(2)}) collective-permute-start(f32[3,16,192]{2,1,0:T(8,128)S(1)} %get-tuple-element.98), channel_id=1, source_target_pairs={{0,16},{16,32},{32,48},{48,64},{64,80},{80,96},{96,112},{112,128},... | collective-permute-start | bytes 110600 | tf_op jit(solution)/shard_map/ppermute | solution.py:24
  82.7 18.8 %collective-permute-start.11 = (f32[22,3,192]{2,1,0:T(4,128)}, f32[22,3,192]{2,1,0:T(4,128)S(1)}, u32[]{:S(2)}, u32[]{:S(2)}) collective-permute-start(f32[22,3,192]{2,1,0:T(4,128)} %get-tuple-element.97), channel_id=1, source_target_pairs={{1,0},{2,1},{3,2},{4,3},{5,4},{6,5},{7,6},{8,7},{9,8},{10,9},{11,1... | collective-permute-start | bytes 152072 | tf_op jit(solution)/shard_map/ppermute | solution.py:25
  84.6 16.9 %collective-permute-start.10 = (f32[22,3,192]{2,1,0:T(4,128)}, f32[22,3,192]{2,1,0:T(4,128)}, u32[]{:S(2)}, u32[]{:S(2)}) collective-permute-start(f32[22,3,192]{2,1,0:T(4,128)} %get-tuple-element.96), channel_id=1, source_target_pairs={{0,1},{1,2},{2,3},{3,4},{4,5},{5,6},{6,7},{7,8},{8,9},{9,10},{10,1... | collective-permute-start | bytes 152072 | tf_op jit(solution)/shard_map/ppermute | solution.py:24
  392.1 33.2 %copy-start.7 = (f32[192,192]{1,0:T(8,128)S(1)}, f32[192,192]{1,0:T(8,128)}, u32[]{:S(2)}) copy-start(f32[192,192]{1,0:T(8,128)} %get-tuple-element.78) | copy-start | bytes 442372
  459.2 53.3 %copy-start.2 = (f32[3,16,16,192]{3,2,1,0:T(8,128)S(1)}, f32[3,16,16,192]{3,2,1,0:T(8,128)}, u32[]{:S(2)}) copy-start(f32[3,16,16,192]{3,2,1,0:T(8,128)} %copy-done.1) | copy-start | bytes 1769476
  (27 other events, 64.1 us)
Sparse Core Ops, SparseCore 0:
  116.8 275.2 all-reduce.9
where the time goes:
time: 628 us; the launch traced here: 619 us
  waiting for transfers between devices  276 us (44%)
  other arithmetic  131 us (21%)
  blocking collectives  95 us (15%)
  starting transfers between devices  38.3 us (6%)
  local copies, waits for them, and re-layouts  31.2 us (5%)
  matrix products  29.5 us (5%)
  between operations  18 us (3%)
    psum x1, waiting for transfers between devices, local(): lax.psum((mass_part, stiff_part), ('slab', 'band'))  275 us
    psum x1, blocking collectives, local(): lax.psum(jnp.einsum('cxym,cxyn->mn', new_modes, new_images, precision=hig...  95 us
    another operation x7, other arithmetic, rotation(): mass_factor = jnp.linalg.cholesky(mass_gram)  29.1 us
    another operation x7, other arithmetic, rotation(): stiff_factor = jnp.linalg.cholesky(projected)  28.7 us
    ppermute x6, starting transfers between devices, padded(): before = lax.ppermute(last, axis, up)  22.2 us
    another operation x4, other arithmetic, rotation(): lax.linalg.triangular_solve(stiff_factor, forward, left_side=True, lower=...  20 us
    another operation x6, other arithmetic, rotation(): lax.linalg.triangular_solve(mass_factor, inverse, left_side=True, lower=T...  19.8 us
    ppermute x6, starting transfers between devices, padded(): after = lax.ppermute(first, axis, down)  16.1 us
  transfers between devices with their start and end apart: 13, of which 2 were waited for; matrix products, arithmetic and copies ran while one was open for 6% of the time, Pallas kernels for 0%

commit v1 on v0

--- a/solution.py
+++ b/solution.py
@@ -199,7 +199,7 @@
     flat_images = image_grid.reshape(-1, column_count)
     stiff_part = jnp.einsum("rk,rl->kl", flat_basis, flat_images, precision=highest)
     mass_part = jnp.einsum("rk,rl->kl", flat_basis, flat_basis, precision=highest)
-    mass_total, stiff_total = lax.psum((mass_part, stiff_part), ("slab", "band"))
+    mass_total, stiff_total = lax.psum(lax.psum((mass_part, stiff_part), "band"), "slab")
     mass_gram = mass_total / total_rows
     stiff_gram = stiff_total / total_rows
     stiff_gram = 0.5 * (stiff_gram + stiff_gram.T)

time: 628 us -> 635 us (1.011)
    psum x1 -> x2, waiting for transfers between devices: 275 us -> 278 us  [the longest x1 155 us: local(): lax.psum(lax.psum((mass_part, stiff_part), 'band'), 'slab')]
  transfers between devices with their start and end apart: 13 -> 14, of which waited for: 2 -> 4; matrix products, arithmetic and copies ran while one was open for 6% -> 6% of each run, Pallas kernels for 0% -> 0%
where the time goes in v1:
time: 635 us; the launch traced here: 626 us
  waiting for transfers between devices  280 us (44%)
  other arithmetic  130 us (20%)
  blocking collectives  101 us (16%)
  starting transfers between devices  38.5 us (6%)
  local copies, waits for them, and re-layouts  29.5 us (5%)
  matrix products  29.5 us (5%)
  between operations  18.1 us (3%)
    psum x1, waiting for transfers between devices, local(): lax.psum(lax.psum((mass_part, stiff_part), 'band'), 'slab')  155 us
    psum x1, waiting for transfers between devices, local(): lax.psum((mass_part, stiff_part), 'band')  123 us
    psum x1, blocking collectives, local(): lax.psum(jnp.einsum('cxym,cxyn->mn', new_modes, new_images, precision=hig...  101 us
    another operation x7, other arithmetic, rotation(): mass_factor = jnp.linalg.cholesky(mass_gram)  28.7 us
    another operation x7, other arithmetic, rotation(): stiff_factor = jnp.linalg.cholesky(projected)  28.7 us
    ppermute x6, starting transfers between devices, padded(): before = lax.ppermute(last, axis, up)  22.2 us
    another operation x6, other arithmetic, rotation(): lax.linalg.triangular_solve(mass_factor, inverse, left_side=True, lower=T...  20.2 us
    another operation x4, other arithmetic, rotation(): lax.linalg.triangular_solve(stiff_factor, forward, left_side=True, lower=...  20 us
  transfers between devices with their start and end apart: 14, of which 4 were waited for; matrix products, arithmetic and copies ran while one was open for 6% of the time, Pallas kernels for 0%

profile of v1, /device:TPU:1, one launch (start us, length us, event | category | flops | bytes accessed | tf_op | source)
XLA Modules:
  0.0 626.2 jit_solution(1652620435558386238)
XLA Ops:
  9.4 4.6 collective-permute-start
  16.1 3.4 collective-permute-start.4
  26.8 7.3 %collective-permute-start.3 = (f32[4,22,3]{2,1,0:T(8,128)}, f32[4,22,3]{2,1,0:T(8,128)S(1)}, u32[]{:S(2)}, u32[]{:S(2)}) collective-permute-start(f32[4,22,3]{2,1,0:T(8,128)} %get-tuple-element.111), channel_id=1, source_target_pairs={{1,0},{2,1},{3,2},{4,3},{5,4},{6,5},{7,6},{8,7},{9,8},{10,9},{11,1... | collective-permute-start | bytes 3176 | tf_op jit(solution)/shard_map/ppermute | solution.py:25
  47.2 3.0 collective-permute-start.7
  61.8 4.4 convolution_subtract_fusion
  69.5 4.9 collective-permute-start.8
  74.4 4.3 fusion.87
  82.3 4.8 collective-permute-start.10
  87.2 4.3 fusion.19
  91.5 5.4 mul.174
  105.6 6.6 %fusion.10 = f32[3,256,192]{1,2,0:T(8,128)S(1)} fusion(f32[3,256,192]{1,2,0:T(8,128)S(1)} %fusion.16, f32[3,256,1452]{1,2,0:T(8,128)} %mul.174, f32[1452,192]{1,0:T(8,128)S(1)} %copy-done, f32[256,3,192]{0,2,1:T(8,128)S(1)} %copy-done.5, f32[3,256,192]{1,2,0:T(8,128)S(1)} %copy-done.6, f32[256]{0:T(256)S(1)} %mul.186), kind=kOutput, calls=%fused_computation.12 | convolution fusion | flops 2569863168 | bytes 7936000 | tf_op jit(solution)/shard_map/dot_general | solution.py:119
  114.6 123.3 %all-reduce.14.cloned.1.call-done = (f32[192,192]{1,0:T(8,128)}, f32[192,192]{1,0:T(8,128)}) async-done(((f32[192,192]{1,0:T(8,128)}, f32[192,192]{1,0:T(8,128)}), (f32[192,192]{1,0:T(8,128)}, f32[192,192]{1,0:T(8,128)})) %all-reduce.14.cloned.1.call-update) | async-done | bytes 294928 | tf_op jit(solution)/shard_map/psum | solution.py:202
  238.3 155.1 %all-reduce.12.cloned.1.call-done = (f32[192,192]{1,0:T(8,128)}, f32[192,192]{1,0:T(8,128)}) async-done(((f32[192,192]{1,0:T(8,128)}, f32[192,192]{1,0:T(8,128)}), (f32[192,192]{1,0:T(8,128)}, f32[192,192]{1,0:T(8,128)})) %all-reduce.12.cloned.1.call-update) | async-done | bytes 294928 | tf_op jit(solution)/shard_map/psum | solution.py:202
  395.5 11.7 %cholesky.171 = f32[128,128]{1,0:T(8,128)S(1)} custom-call(f32[128,128]{1,0:T(8,128)S(1)} %copy.93), custom_call_target="Cholesky" | custom-call | tf_op jit(solution)/shard_map/jit(cholesky)/cholesky | solution.py:135
  407.3 9.8 %custom-call.28 = f32[1,128,128]{1,2,0:T(8,128)S(1)} custom-call(f32[1,128,128]{2,1,0:T(8,128)S(1)} %get-tuple-element.105), custom_call_target="InvertDiagBlocksLowerTriangular" | custom-call | tf_op jit(solution)/shard_map/jit(cholesky)/cholesky | solution.py:135
  417.7 5.9 cholesky.191
  426.5 20.1 %custom-call.33 = f32[2,128,128]{1,2,0:T(8,128)S(1)} custom-call(f32[2,128,128]{2,1,0:T(8,128)S(1)} %pad_maximum_fusion.4), custom_call_target="InvertDiagBlocksLowerTriangular" | custom-call | tf_op jit(solution)/shard_map/triangular_solve/custom-call.6 | solution.py:146
  448.8 11.7 %cholesky.209 = f32[128,128]{1,0:T(8,128)S(1)} custom-call(f32[128,128]{1,0:T(8,128)S(1)} %cholesky.246), custom_call_target="Cholesky" | custom-call | tf_op jit(solution)/shard_map/jit(cholesky)/cholesky | solution.py:139
  460.5 9.8 %custom-call.31 = f32[1,128,128]{1,2,0:T(8,128)S(1)} custom-call(f32[1,128,128]{2,1,0:T(8,128)S(1)} %get-tuple-element.103), custom_call_target="InvertDiagBlocksLowerTriangular" | custom-call | tf_op jit(solution)/shard_map/jit(cholesky)/cholesky | solution.py:139
  470.7 5.8 cholesky.229
  479.4 19.8 %custom-call.32 = f32[2,128,128]{1,2,0:T(8,128)S(1)} custom-call(f32[2,128,128]{2,1,0:T(8,128)S(1)} %pad_maximum_fusion.5), custom_call_target="InvertDiagBlocksLowerTriangular" | custom-call | tf_op jit(solution)/shard_map/triangular_solve/custom-call.6 | solution.py:142
  501.4 5.8 cholesky.98
  508.6 4.9 custom-call.24
  517.8 100.8 %psum.39 = f32[64,64]{1,0:T(8,128)S(1)} all-reduce(f32[64,64]{1,0:T(8,128)S(1)} %convolution_bitcast_fusion.3), channel_id=1, replica_groups=mesh['slab'=32,'band'=16] {'slab','band'}, use_global_device_ids=true, to_apply=%region_14.18 | all-reduce | flops 4096 | bytes 32768 | tf_op jit(solution)/shard_map/psum | solution.py:210
  (230 shorter events, 70.6 us)
Async XLA Ops:
  7.2 13.6 %copy-start.8 = (f32[3,16,16]{2,1,0:T(8,128)S(1)}, f32[3,16,16]{2,1,0:T(8,128)}, u32[]{:S(2)}) copy-start(f32[3,16,16]{2,1,0:T(8,128)} %param.12) | copy-start | bytes 9220
  7.2 14.2 %copy-start.3 = (f32[3,16,3072]{2,1,0:T(8,128)S(1)}, f32[3,16,3072]{2,1,0:T(8,128)}, u32[]{:S(2)}) copy-start(f32[3,16,3072]{2,1,0:T(8,128)} %param.11) | copy-start | bytes 1769476
  7.2 230.7 %all-reduce.14.cloned.1.call-start = ((), (), s32[]{:S(2)}) async-start(), calls=%async_computation.1 | async-start | bytes 786432 | tf_op jit(solution)/shard_map/psum | solution.py:202
  8.1 18.1 %collective-permute-start.1 = (f32[4,3,16]{2,1,0:T(4,128)S(1)}, f32[4,3,16]{2,1,0:T(4,128)S(1)}, u32[]{:S(2)}, u32[]{:S(2)}) collective-permute-start(f32[4,3,16]{2,1,0:T(4,128)S(1)} %get-tuple-element.117), channel_id=1, source_target_pairs={{16,0},{32,16},{48,32},{64,48},{80,64},{96,80},{112,96},{128,112},... | collective-permute-start | bytes 2312 | tf_op jit(solution)/shard_map/ppermute | solution.py:25
  9.3 13.2 %copy-start.34 = (s32[1,2,9]{2,1,0:T(2,128)S(1)}, s32[1,2,9]{2,1,0:T(2,128)}, u32[]{:S(2)}) copy-start(s32[1,2,9]{2,1,0:T(2,128)} %param.16) | copy-start | bytes 220
  9.3 14.4 %copy-start.20 = (f32[16,16]{1,0:T(8,128)S(1)}, f32[16,16]{1,0:T(8,128)}, u32[]{:S(2)}) copy-start(f32[16,16]{1,0:T(8,128)} %param.14) | copy-start | bytes 3076
  9.4 16.8 %collective-permute-start = (f32[4,3,16]{2,1,0:T(4,128)S(1)}, f32[4,3,16]{2,1,0:T(4,128)S(1)}, u32[]{:S(2)}, u32[]{:S(2)}) collective-permute-start(f32[4,3,16]{2,1,0:T(4,128)S(1)} %get-tuple-element.116), channel_id=1, source_target_pairs={{0,16},{16,32},{32,48},{48,64},{64,80},{80,96},{96,112},{112,128},... | collective-permute-start | bytes 2312 | tf_op jit(solution)/shard_map/ppermute | solution.py:24
  15.4 30.7 %copy-start.1 = (f32[3,16,16,192]{3,2,1,0:T(8,128)}, f32[3,16,16,192]{3,2,1,0:T(8,128)S(1)}, u32[]{:S(2)}) copy-start(f32[3,16,16,192]{3,2,1,0:T(8,128)S(1)} %reshape.1000) | copy-start | bytes 1769476
  16.1 29.9 %collective-permute-start.4 = (f32[3,3,16,192]{3,2,1,0:T(8,128)}, f32[3,3,16,192]{3,2,1,0:T(8,128)S(1)}, u32[]{:S(2)}, u32[]{:S(2)}) collective-permute-start(f32[3,3,16,192]{3,2,1,0:T(8,128)} %get-tuple-element.95), channel_id=1, source_target_pairs={{0,16},{16,32},{32,48},{48,64},{64,80},{80,96},{96,112},{112,128},... | collective-permute-start | bytes 331784 | tf_op jit(solution)/shard_map/ppermute | solution.py:24
  19.5 26.7 %collective-permute-start.5 = (f32[3,3,16,192]{3,2,1,0:T(8,128)S(1)}, f32[3,3,16,192]{3,2,1,0:T(8,128)S(1)}, u32[]{:S(2)}, u32[]{:S(2)}) collective-permute-start(f32[3,3,16,192]{3,2,1,0:T(8,128)S(1)} %get-tuple-element.94), channel_id=1, source_target_pairs={{16,0},{32,16},{48,32},{64,48},{80,64},{96,80},{112,96},{128,112},... | collective-permute-start | bytes 331784 | tf_op jit(solution)/shard_map/ppermute | solution.py:25
  26.0 10.7 %copy-start.10 = (s32[484]{0:T(512)}, s32[484]{0:T(512)S(1)}, u32[]{:S(2)}) copy-start(s32[484]{0:T(512)S(1)} %sub.437) | copy-start | bytes 5812
  26.1 10.5 %copy-start.12 = (s32[484]{0:T(512)}, s32[484]{0:T(512)S(1)}, u32[]{:S(2)}) copy-start(s32[484]{0:T(512)S(1)} %sub.429) | copy-start | bytes 5812
  26.8 14.4 %collective-permute-start.3 = (f32[4,22,3]{2,1,0:T(8,128)}, f32[4,22,3]{2,1,0:T(8,128)S(1)}, u32[]{:S(2)}, u32[]{:S(2)}) collective-permute-start(f32[4,22,3]{2,1,0:T(8,128)} %get-tuple-element.111), channel_id=1, source_target_pairs={{1,0},{2,1},{3,2},{4,3},{5,4},{6,5},{7,6},{8,7},{9,8},{10,9},{11,1... | collective-permute-start | bytes 3176 | tf_op jit(solution)/shard_map/ppermute | solution.py:25
  34.1 7.1 %collective-permute-start.2 = (f32[4,22,3]{2,1,0:T(8,128)S(1)}, f32[4,22,3]{2,1,0:T(8,128)}, u32[]{:S(2)}, u32[]{:S(2)}) collective-permute-start(f32[4,22,3]{2,1,0:T(8,128)S(1)} %get-tuple-element.110), channel_id=1, source_target_pairs={{0,1},{1,2},{2,3},{3,4},{4,5},{5,6},{6,7},{7,8},{8,9},{9,10},{10,1... | collective-permute-start | bytes 3176 | tf_op jit(solution)/shard_map/ppermute | solution.py:24
  46.2 6.6 %copy-start.4 = (f32[3,22,16,192]{3,2,1,0:T(8,128)}, f32[3,22,16,192]{3,2,1,0:T(8,128)S(1)}, u32[]{:S(2)}) copy-start(f32[3,22,16,192]{3,2,1,0:T(8,128)S(1)} %constant_dynamic-update-slice_fusion) | copy-start | bytes 2433028
  47.2 8.1 %collective-permute-start.7 = (f32[3,22,3,192]{3,2,1,0:T(4,128)}, f32[3,22,3,192]{3,2,1,0:T(4,128)}, u32[]{:S(2)}, u32[]{:S(2)}) collective-permute-start(f32[3,22,3,192]{3,2,1,0:T(4,128)} %get-tuple-element.93), channel_id=1, source_target_pairs={{1,0},{2,1},{3,2},{4,3},{5,4},{6,5},{7,6},{8,7},{9,8},{10,9},{11,1... | collective-permute-start | bytes 456200 | tf_op jit(solution)/shard_map/ppermute | solution.py:25
  50.2 6.3 %collective-permute-start.6 = (f32[3,22,3,192]{3,2,1,0:T(4,128)}, f32[3,22,3,192]{3,2,1,0:T(4,128)}, u32[]{:S(2)}, u32[]{:S(2)}) collective-permute-start(f32[3,22,3,192]{3,2,1,0:T(4,128)} %get-tuple-element.92), channel_id=1, source_target_pairs={{0,1},{1,2},{2,3},{3,4},{4,5},{5,6},{6,7},{7,8},{8,9},{9,10},{10,1... | collective-permute-start | bytes 456200 | tf_op jit(solution)/shard_map/ppermute | solution.py:24
  68.2 11.5 %collective-permute-start.9 = (f32[3,16,192]{2,1,0:T(8,128)S(1)}, f32[3,16,192]{2,1,0:T(8,128)S(1)}, u32[]{:S(2)}, u32[]{:S(2)}) collective-permute-start(f32[3,16,192]{2,1,0:T(8,128)S(1)} %get-tuple-element.101), channel_id=1, source_target_pairs={{16,0},{32,16},{48,32},{64,48},{80,64},{96,80},{112,96},{128,112},... | collective-permute-start | bytes 110600 | tf_op jit(solution)/shard_map/ppermute | solution.py:25
  69.5 10.2 %collective-permute-start.8 = (f32[3,16,192]{2,1,0:T(8,128)S(1)}, f32[3,16,192]{2,1,0:T(8,128)S(1)}, u32[]{:S(2)}, u32[]{:S(2)}) collective-permute-start(f32[3,16,192]{2,1,0:T(8,128)S(1)} %get-tuple-element.100), channel_id=1, source_target_pairs={{0,16},{16,32},{32,48},{48,64},{64,80},{80,96},{96,112},{112,128},... | collective-permute-start | bytes 110600 | tf_op jit(solution)/shard_map/ppermute | solution.py:24
  80.4 18.8 %collective-permute-start.11 = (f32[22,3,192]{2,1,0:T(4,128)}, f32[22,3,192]{2,1,0:T(4,128)S(1)}, u32[]{:S(2)}, u32[]{:S(2)}) collective-permute-start(f32[22,3,192]{2,1,0:T(4,128)} %get-tuple-element.99), channel_id=1, source_target_pairs={{1,0},{2,1},{3,2},{4,3},{5,4},{6,5},{7,6},{8,7},{9,8},{10,9},{11,1... | collective-permute-start | bytes 152072 | tf_op jit(solution)/shard_map/ppermute | solution.py:25
  82.3 16.9 %collective-permute-start.10 = (f32[22,3,192]{2,1,0:T(4,128)}, f32[22,3,192]{2,1,0:T(4,128)}, u32[]{:S(2)}, u32[]{:S(2)}) collective-permute-start(f32[22,3,192]{2,1,0:T(4,128)} %get-tuple-element.98), channel_id=1, source_target_pairs={{0,1},{1,2},{2,3},{3,4},{4,5},{5,6},{6,7},{7,8},{8,9},{9,10},{10,1... | collective-permute-start | bytes 152072 | tf_op jit(solution)/shard_map/ppermute | solution.py:24
  114.4 279.0 %all-reduce.12.cloned.1.call-start = ((), (), s32[]{:S(2)}) async-start(), calls=%async_computation | async-start | bytes 786432 | tf_op jit(solution)/shard_map/psum | solution.py:202
  393.4 32.8 %copy-start.7 = (f32[192,192]{1,0:T(8,128)S(1)}, f32[192,192]{1,0:T(8,128)}, u32[]{:S(2)}) copy-start(f32[192,192]{1,0:T(8,128)} %get-tuple-element.78) | copy-start | bytes 442372
  460.5 53.3 %copy-start.2 = (f32[3,16,16,192]{3,2,1,0:T(8,128)S(1)}, f32[3,16,16,192]{3,2,1,0:T(8,128)}, u32[]{:S(2)}) copy-start(f32[3,16,16,192]{3,2,1,0:T(8,128)} %copy-done.1) | copy-start | bytes 1769476
  (25 other events, 52.2 us)
Sparse Core Ops, SparseCore 0:
  114.5 123.3 all-reduce.13
  241.7 151.5 all-reduce.11
